TPU v7x, 32 devices: a whole 2x2x4 slice. The times are simulated.
32 devices in a mesh: row: 8 (over z, y), col: 4 (over x, core).
Axes of the slice: x: 2, y: 2, z: 4, core: 2. Of those that a mesh axis runs over, the one named last changes fastest.
Arguments:
- factor: float32 [2, 1024, 1024], P(None, 'row', 'col'), may hold values from -0.125 to 0.125
- lower_inverse: float32 [2, 512, 1024], P(None, None, 'row'), may hold values from -1 to 2
- upper_inverse: float32 [2, 512, 1024], P(None, None, 'row'), may hold values from -1 to 2
- krylov_block: float32 [2, 16, 1024], P(None, None, 'row'), may hold values from -6 to 6
- basis: float32 [2, 64, 1024], P(None, None, 'row'), may hold values from -0.125 to 0.125
Outputs:
- projected: float32 [2, 16, 1024], P(None, None, 'row')
- coefficients: float32 [2, 64, 16], replicated
All inputs are finite; a program needn't handle non-finite values.
Results may differ from a plain program's by a relative error of at most 0.00012.
Values sent between devices are 32-bit elements; how exact they have to be, the bound alone decides.
A program may use at most 64 MiB of HBM per device.

v0:
```python
import jax
import jax.numpy as jnp
from jax import lax
from jax.sharding import PartitionSpec as P


def real_dot(left, right):
    return jnp.dot(left, right, preferred_element_type=jnp.float32, precision=lax.Precision.HIGHEST)


def apply_tile(matrix, vectors):
    real_part = real_dot(vectors[0], matrix[0].T) - real_dot(vectors[1], matrix[1].T)
    imag_part = real_dot(vectors[0], matrix[1].T) + real_dot(vectors[1], matrix[0].T)
    return jnp.stack([real_part, imag_part])


def herm_dot(basis_part, vectors):
    real_part = real_dot(basis_part[0], vectors[0].T) + real_dot(basis_part[1], vectors[1].T)
    imag_part = real_dot(basis_part[0], vectors[1].T) - real_dot(basis_part[1], vectors[0].T)
    return jnp.stack([real_part, imag_part])


def combine(basis_part, coeffs):
    real_part = real_dot(coeffs[0].T, basis_part[0]) - real_dot(coeffs[1].T, basis_part[1])
    imag_part = real_dot(coeffs[0].T, basis_part[1]) + real_dot(coeffs[1].T, basis_part[0])
    return jnp.stack([real_part, imag_part])


def small_product(gram, coeffs):
    real_part = real_dot(gram[0], coeffs[0]) - real_dot(gram[1], coeffs[1])
    imag_part = real_dot(gram[0], coeffs[1]) + real_dot(gram[1], coeffs[0])
    return jnp.stack([real_part, imag_part])


def local(factor, lower_inverse, upper_inverse, krylov_block, basis):
    tile = lower_inverse.shape[1]
    rows_local = factor.shape[1]
    width = factor.shape[2]
    nvec = krylov_block.shape[1]
    share = tile // rows_local
    tiles = lax.axis_size("row") // share
    row_idx = lax.axis_index("row")
    col_idx = lax.axis_index("col")
    own_tile = row_idx // share
    piece_idx = row_idx % share

    def sweep(inverse, pick, backward):
        start = jnp.zeros((2, nvec, tiles * tile), jnp.float32)

        def step(index, current):
            k = tiles - 1 - index if backward else index
            k = jnp.asarray(k).astype(jnp.int32)
            owner = own_tile == k
            cols = lax.dynamic_slice_in_dim(current, col_idx * width, width, 2)
            partial_value = apply_tile(factor, cols)
            given = pick(k)
            summed = lax.psum(partial_value, "col")
            term = apply_tile(inverse, given - summed)
            term = jnp.where(owner, term, jnp.zeros_like(term))
            piece = lax.psum(term, "row")
            return lax.dynamic_update_slice_in_dim(current, piece, k * tile, 2)

        return lax.fori_loop(0, tiles, step, start)

    def pick_forward(k):
        return krylov_block

    solved = sweep(lower_inverse, pick_forward, False)

    def pick_backward(k):
        return lax.dynamic_slice_in_dim(solved, k * tile + piece_idx * rows_local, rows_local, 2)

    solution = sweep(upper_inverse, pick_backward, True)
    own_rows = lax.dynamic_slice_in_dim(solution, row_idx * rows_local, rows_local, 2)
    local_first = herm_dot(basis, own_rows)
    first, gram = lax.psum((local_first, herm_dot(basis, basis)), "row")
    middle = own_rows - combine(basis, first)
    second = first - small_product(gram, first)
    projected = middle - combine(basis, second)
    return (projected, first + second)


def solution(mesh):
    in_specs = (
        P(None, "row", "col"),
        P(None, None, "row"),
        P(None, None, "row"),
        P(None, None, "row"),
        P(None, None, "row"),
    )
    out_specs = (P(None, None, "row"), P())
    return jax.shard_map(local, mesh=mesh, in_specs=in_specs, out_specs=out_specs, check_vma=False)
```

profile of v0, /device:TPU:0, one launch (start us, length us, event | category | flops | bytes accessed | tf_op | source)
XLA Modules:
  0.0 401.9 jit_solution(1856466188070907710)
XLA Ops:
  7.2 0.7 copy-done.5
  7.9 175.2 %while.30 = (s32[]{:T(128)}, f32[2,16,1024]{2,1,0:T(8,128)S(1)}, s32[]{:T(128)}, s32[]{:T(128)}, f32[2,128,256]{2,1,0:T(8,128)}, /*index=5*/f32[2,16,128]{2,1,0:...) while((s32[]{:T(128)}, f32[2,16,1024]{2,1,0:T(8,128)S(1)}, ...), condition=%wide.region_3.4_spmd, body=%wide.region_0.3_spmd.sunk | while | flops 75579392 | bytes 5834029 | solution.py:63
  7.9 1.2 fusion.158
  9.1 1.1 fusion.160
  10.4 0.2 fusion.161
  10.7 12.7 %psum.72 = f32[2,16,128]{2,1,0:T(8,128)S(1)} all-reduce(f32[2,16,128]{2,1,0:T(8,128)S(1)} %pad_maximum_fusion.6), channel_id=1, replica_groups=mesh['row'=8,'col'=4] {'col'}, use_global_device_ids=true, to_apply=%region_1.1 | all-reduce | flops 4096 | bytes 32768 | tf_op jit(solution)/shard_map/while/body/eval_jaxpr/psum | solution.py:57
  23.4 1.3 fusion.164
  24.7 0.3 fusion.162
  25.0 0.3 fusion.165
  25.3 0.3 fusion.163
  25.6 0.6 maximum_select_fusion.4
  26.3 69.7 %all-reduce.4.cloned.1.call-done = f32[2,16,512]{2,1,0:T(8,128)} async-done(((f32[2,16,512]{2,1,0:T(8,128)}), f32[2,16,512]{2,1,0:T(8,128)}) %all-reduce.4.cloned.1.call-update) | async-done | bytes 65552 | tf_op jit(solution)/shard_map/while/body/eval_jaxpr/psum | solution.py:60
  96.0 0.8 constant_dynamic-update-slice_fusion.4
  96.9 1.1 fusion.158
  98.1 1.1 fusion.160
  99.4 0.2 fusion.161
  99.7 10.1 %psum.72 = f32[2,16,128]{2,1,0:T(8,128)S(1)} all-reduce(f32[2,16,128]{2,1,0:T(8,128)S(1)} %pad_maximum_fusion.6), channel_id=1, replica_groups=mesh['row'=8,'col'=4] {'col'}, use_global_device_ids=true, to_apply=%region_1.1 | all-reduce | flops 4096 | bytes 32768 | tf_op jit(solution)/shard_map/while/body/eval_jaxpr/psum | solution.py:57
  109.8 1.3 fusion.164
  111.1 0.3 fusion.162
  111.4 0.3 fusion.165
  111.7 0.3 fusion.163
  112.1 0.6 maximum_select_fusion.4
  112.7 69.5 %all-reduce.4.cloned.1.call-done = f32[2,16,512]{2,1,0:T(8,128)} async-done(((f32[2,16,512]{2,1,0:T(8,128)}), f32[2,16,512]{2,1,0:T(8,128)}) %all-reduce.4.cloned.1.call-update) | async-done | bytes 65552 | tf_op jit(solution)/shard_map/while/body/eval_jaxpr/psum | solution.py:60
  182.2 0.8 constant_dynamic-update-slice_fusion.4
  183.1 170.5 %while.31 = (s32[]{:T(128)}, f32[2,16,1024]{2,1,0:T(8,128)S(1)}, s32[]{:T(128)}, s32[]{:T(128)}, f32[2,16,1024]{2,1,0:T(8,128)S(1)}, /*index=5*/s32[]{:T(128)}, ...) while((s32[]{:T(128)}, f32[2,16,1024]{2,1,0:T(8,128)S(1)}, ...), condition=%wide.region_7.8_spmd, body=%wide.region_4.7_spmd.sunk | while | flops 75579392 | bytes 5834099 | solution.py:63
  183.2 1.1 fusion.174
  184.3 1.1 fusion.176
  185.9 10.1 %psum.74 = f32[2,16,128]{2,1,0:T(8,128)S(1)} all-reduce(f32[2,16,128]{2,1,0:T(8,128)S(1)} %pad_maximum_fusion.7), channel_id=1, replica_groups=mesh['row'=8,'col'=4] {'col'}, use_global_device_ids=true, to_apply=%region_5.5 | all-reduce | flops 4096 | bytes 32768 | tf_op jit(solution)/shard_map/while/body/eval_jaxpr/psum | solution.py:57
  196.1 0.3 fusion.180
  196.4 0.3 fusion.178
  196.7 0.3 fusion.181
  197.0 0.3 fusion.179
  197.4 0.6 maximum_select_fusion.5
  198.0 69.5 %all-reduce.6.cloned.1.call-done = f32[2,16,512]{2,1,0:T(8,128)} async-done(((f32[2,16,512]{2,1,0:T(8,128)}), f32[2,16,512]{2,1,0:T(8,128)}) %all-reduce.6.cloned.1.call-update) | async-done | bytes 65552 | tf_op jit(solution)/shard_map/while/body/eval_jaxpr/psum | solution.py:60
  267.5 0.8 constant_dynamic-update-slice_fusion.5
  268.4 1.1 fusion.174
  269.6 1.1 fusion.176
  271.2 10.1 %psum.74 = f32[2,16,128]{2,1,0:T(8,128)S(1)} all-reduce(f32[2,16,128]{2,1,0:T(8,128)S(1)} %pad_maximum_fusion.7), channel_id=1, replica_groups=mesh['row'=8,'col'=4] {'col'}, use_global_device_ids=true, to_apply=%region_5.5 | all-reduce | flops 4096 | bytes 32768 | tf_op jit(solution)/shard_map/while/body/eval_jaxpr/psum | solution.py:57
  281.3 0.3 fusion.180
  281.6 0.3 fusion.178
  282.0 0.3 fusion.181
  282.3 0.3 fusion.179
  282.6 0.6 maximum_select_fusion.5
  283.3 69.5 %all-reduce.6.cloned.1.call-done = f32[2,16,512]{2,1,0:T(8,128)} async-done(((f32[2,16,512]{2,1,0:T(8,128)}), f32[2,16,512]{2,1,0:T(8,128)}) %all-reduce.6.cloned.1.call-update) | async-done | bytes 65552 | tf_op jit(solution)/shard_map/while/body/eval_jaxpr/psum | solution.py:60
  352.8 0.8 constant_dynamic-update-slice_fusion.5
  355.1 37.1 %all-reduce = (f32[2,64,16]{1,2,0:T(8,128)S(1)}, f32[2,64,64]{2,1,0:T(8,128)S(1)}) all-reduce(f32[2,64,16]{1,2,0:T(8,128)S(1)} %pad_maximum_fusion.3, f32[2,64,64]{2,1,0:T(8,128)S(1)} %pad_maximum_fusion.2), channel_id=1, replica_groups=mesh['row'=8,'col'=4] {'row'}, use_global_device_ids=true, to_apply=%region_8.9 | all-reduce | flops 10240 | bytes 81920 | tf_op jit(solution)/shard_map/psum | solution.py:76
  392.9 0.6 fusion.117
  394.7 0.6 fusion.112
  (65 shorter events, 4.9 us)
Async XLA Ops:
  7.2 0.7 copy-start.5
  7.9 345.7 %copy-start.4 = (f32[2,64,128]{2,1,0:T(8,128)S(1)}, f32[2,64,128]{2,1,0:T(8,128)}, u32[]{:S(2)}) copy-start(f32[2,64,128]{2,1,0:T(8,128)} %param.13) | copy-start | bytes 196612
  7.9 2.3 copy-start
  7.9 88.1 %all-reduce.4.cloned.1.call-start = ((), (), s32[]{:S(2)}) async-start(), calls=%async_computation | async-start | bytes 131072 | tf_op jit(solution)/shard_map/while/body/eval_jaxpr/psum | solution.py:60
  7.9 16.8 %copy-start.2 = (f32[2,512,128]{2,1,0:T(8,128)S(1)}, f32[2,512,128]{2,1,0:T(8,128)}, u32[]{:S(2)}) copy-start(f32[2,512,128]{2,1,0:T(8,128)} %get-tuple-element.529) | copy-start | bytes 1572868 | tf_op jit(solution)/shard_map/while
  96.9 2.4 copy-start
  96.9 85.4 %all-reduce.4.cloned.1.call-start = ((), (), s32[]{:S(2)}) async-start(), calls=%async_computation | async-start | bytes 131072 | tf_op jit(solution)/shard_map/while/body/eval_jaxpr/psum | solution.py:60
  96.9 14.2 %copy-start.2 = (f32[2,512,128]{2,1,0:T(8,128)S(1)}, f32[2,512,128]{2,1,0:T(8,128)}, u32[]{:S(2)}) copy-start(f32[2,512,128]{2,1,0:T(8,128)} %get-tuple-element.529) | copy-start | bytes 1572868 | tf_op jit(solution)/shard_map/while
  183.1 2.4 copy-start.1
  183.1 13.0 %copy-start.3 = (f32[2,512,128]{2,1,0:T(8,128)S(1)}, f32[2,512,128]{2,1,0:T(8,128)}, u32[]{:S(2)}) copy-start(f32[2,512,128]{2,1,0:T(8,128)} %get-tuple-element.568) | copy-start | bytes 1572868 | tf_op jit(solution)/shard_map/while
  183.1 84.4 %all-reduce.6.cloned.1.call-start = ((), (), s32[]{:S(2)}) async-start(), calls=%async_computation.1 | async-start | bytes 131072 | tf_op jit(solution)/shard_map/while/body/eval_jaxpr/psum | solution.py:60
  268.4 2.4 copy-start.1
  268.4 13.0 %copy-start.3 = (f32[2,512,128]{2,1,0:T(8,128)S(1)}, f32[2,512,128]{2,1,0:T(8,128)}, u32[]{:S(2)}) copy-start(f32[2,512,128]{2,1,0:T(8,128)} %get-tuple-element.568) | copy-start | bytes 1572868 | tf_op jit(solution)/shard_map/while
  268.4 84.4 %all-reduce.6.cloned.1.call-start = ((), (), s32[]{:S(2)}) async-start(), calls=%async_computation.1 | async-start | bytes 131072 | tf_op jit(solution)/shard_map/while/body/eval_jaxpr/psum | solution.py:60
Sparse Core Ops, SparseCore 0:
  26.4 69.5 all-reduce.3
  112.8 69.3 all-reduce.3
  198.1 69.3 all-reduce.5
  283.4 69.3 all-reduce.5
where the time goes:
time: 403 us; the launch traced here: 402 us
  waiting for transfers between devices  278 us (69%)
  blocking collectives  80.2 us (20%)
  matrix products  20.8 us (5%)
  between operations  13.8 us (3%)
  local copies, waits for them, and re-layouts  4.26 us (1%)
  other arithmetic  4.03 us (1%)
    psum x4, waiting for transfers between devices, step(): piece = lax.psum(term, 'row')  278 us
    psum x4, blocking collectives, step(): summed = lax.psum(partial_value, 'col')  43 us
    psum x1, blocking collectives, local(): first, gram = lax.psum((local_first, herm_dot(basis, basis)), 'row')  37.1 us
    dot_general x52, matrix products, real_dot(): jnp.dot(left, right, preferred_element_type=jnp.float32, precision=lax.Pr...  20.8 us
  transfers between devices with their start and end apart: 4, of which 4 were waited for; matrix products, arithmetic and copies ran while one was open for 0% of the time, Pallas kernels for 0%

commit v1 on v0

--- a/solution.py
+++ b/solution.py
@@ -57,7 +57,7 @@
             summed = lax.psum(partial_value, "col")
             term = apply_tile(inverse, given - summed)
             term = jnp.where(owner, term, jnp.zeros_like(term))
-            piece = lax.psum(term, "row")
+            piece = jnp.sum(lax.all_gather(term, "row"), axis=0)
             return lax.dynamic_update_slice_in_dim(current, piece, k * tile, 2)
 
         return lax.fori_loop(0, tiles, step, start)

time: 403 us -> 233 us (0.58)
  waiting for transfers between devices: 278 us -> 0 us
  blocking collectives: 80.2 us -> 208 us
  between operations: 13.8 us -> 0.78 us
    psum x4 -> x0, waiting for transfers between devices: 278 us -> none  [step(): piece = lax.psum(term, 'row')]
    all_gather x0 -> x4, blocking collectives: none -> 127 us  [step(): piece = jnp.sum(lax.all_gather(term, 'row'), axis=0)]
  transfers between devices with their start and end apart: 4 -> 0, of which waited for: 4 -> 0; matrix products, arithmetic and copies ran while one was open for 0% -> 0% of each run, Pallas kernels for 0% -> 0%
where the time goes in v1:
time: 233 us
  blocking collectives  208 us (89%)
  matrix products  21 us (9%)
    all_gather x4, blocking collectives, step(): piece = jnp.sum(lax.all_gather(term, 'row'), axis=0)  127 us
    psum x4, blocking collectives, step(): summed = lax.psum(partial_value, 'col')  43 us
    psum x1, blocking collectives, local(): first, gram = lax.psum((local_first, herm_dot(basis, basis)), 'row')  38.1 us
    dot_general x52, matrix products, real_dot(): jnp.dot(left, right, preferred_element_type=jnp.float32, precision=lax.Pr...  21 us

profile of v1, /device:TPU:0, one launch (start us, length us, event | category | flops | bytes accessed | tf_op | source)
XLA Modules:
  0.0 232.5 jit_solution(85409113866405114)
XLA Ops:
  0.7 0.7 copy-done.5
  1.4 96.6 %while.30 = (s32[]{:T(128)}, f32[2,16,1024]{2,1,0:T(8,128)S(1)}, s32[]{:T(128)}, s32[]{:T(128)}, f32[2,128,256]{2,1,0:T(8,128)}, /*index=5*/f32[2,16,128]{2,1,0:...) while((s32[]{:T(128)}, f32[2,16,1024]{2,1,0:T(8,128)S(1)}, ...), condition=%wide.region_3.4_spmd, body=%wide.region_0.3_spmd.sunk | while | flops 75677696 | bytes 6620433 | solution.py:63
  1.4 1.2 fusion.158
  2.5 1.1 fusion.159
  3.9 0.2 fusion.161
  4.2 12.7 %psum.44 = f32[2,16,128]{2,1,0:T(8,128)S(1)} all-reduce(f32[2,16,128]{2,1,0:T(8,128)S(1)} %pad_maximum_fusion.6), channel_id=1, replica_groups=mesh['row'=8,'col'=4] {'col'}, use_global_device_ids=true, to_apply=%region_1.1 | all-reduce | flops 4096 | bytes 32768 | tf_op jit(solution)/shard_map/while/body/eval_jaxpr/psum | solution.py:57
  16.9 1.3 fusion.164
  18.1 0.3 fusion.165
  18.4 0.3 fusion.162
  18.8 0.3 fusion.163
  19.1 32.0 %all_gather.26 = f32[8,2,16,512]{3,2,1,0:T(8,128)S(1)} all-gather(f32[1,2,16,512]{3,2,1,0:T(8,128)S(1)} %maximum_select_fusion.4), channel_id=1, replica_groups=mesh['row'=8,'col'=4] {'row'}, dimensions={0}, use_global_device_ids=true | all-gather | bytes 589824 | tf_op jit(solution)/shard_map/while/body/eval_jaxpr/all_gather | solution.py:60
  51.2 1.2 fusion.158
  52.3 1.1 fusion.159
  53.7 0.2 fusion.161
  54.0 10.1 %psum.44 = f32[2,16,128]{2,1,0:T(8,128)S(1)} all-reduce(f32[2,16,128]{2,1,0:T(8,128)S(1)} %pad_maximum_fusion.6), channel_id=1, replica_groups=mesh['row'=8,'col'=4] {'col'}, use_global_device_ids=true, to_apply=%region_1.1 | all-reduce | flops 4096 | bytes 32768 | tf_op jit(solution)/shard_map/while/body/eval_jaxpr/psum | solution.py:57
  64.1 1.3 fusion.164
  65.4 0.3 fusion.165
  65.7 0.3 fusion.162
  66.0 0.3 fusion.163
  66.4 31.6 %all_gather.26 = f32[8,2,16,512]{3,2,1,0:T(8,128)S(1)} all-gather(f32[1,2,16,512]{3,2,1,0:T(8,128)S(1)} %maximum_select_fusion.4), channel_id=1, replica_groups=mesh['row'=8,'col'=4] {'row'}, dimensions={0}, use_global_device_ids=true | all-gather | bytes 589824 | tf_op jit(solution)/shard_map/while/body/eval_jaxpr/all_gather | solution.py:60
  98.0 91.8 %while.31 = (s32[]{:T(128)}, f32[2,16,1024]{2,1,0:T(8,128)S(1)}, s32[]{:T(128)}, s32[]{:T(128)}, f32[2,16,1024]{2,1,0:T(8,128)S(1)}, /*index=5*/s32[]{:T(128)}, ...) while((s32[]{:T(128)}, f32[2,16,1024]{2,1,0:T(8,128)S(1)}, ...), condition=%wide.region_7.8_spmd, body=%wide.region_4.7_spmd.sunk | while | flops 75677696 | bytes 6620503 | solution.py:63
  98.1 1.2 fusion.174
  99.2 1.1 fusion.175
  100.6 0.2 fusion.177
  100.9 10.1 %psum.45 = f32[2,16,128]{2,1,0:T(8,128)S(1)} all-reduce(f32[2,16,128]{2,1,0:T(8,128)S(1)} %pad_maximum_fusion.7), channel_id=1, replica_groups=mesh['row'=8,'col'=4] {'col'}, use_global_device_ids=true, to_apply=%region_5.5 | all-reduce | flops 4096 | bytes 32768 | tf_op jit(solution)/shard_map/while/body/eval_jaxpr/psum | solution.py:57
  111.0 0.3 fusion.180
  111.3 0.3 fusion.181
  111.6 0.3 fusion.178
  112.0 0.3 fusion.179
  112.3 31.5 %all_gather.27 = f32[8,2,16,512]{3,2,1,0:T(8,128)S(1)} all-gather(f32[1,2,16,512]{3,2,1,0:T(8,128)S(1)} %maximum_select_fusion.5), channel_id=1, replica_groups=mesh['row'=8,'col'=4] {'row'}, dimensions={0}, use_global_device_ids=true | all-gather | bytes 589824 | tf_op jit(solution)/shard_map/while/body/eval_jaxpr/all_gather | solution.py:60
  143.9 1.2 fusion.174
  145.1 1.1 fusion.175
  146.3 0.2 fusion.176
  146.4 0.2 fusion.177
  146.7 10.1 %psum.45 = f32[2,16,128]{2,1,0:T(8,128)S(1)} all-reduce(f32[2,16,128]{2,1,0:T(8,128)S(1)} %pad_maximum_fusion.7), channel_id=1, replica_groups=mesh['row'=8,'col'=4] {'col'}, use_global_device_ids=true, to_apply=%region_5.5 | all-reduce | flops 4096 | bytes 32768 | tf_op jit(solution)/shard_map/while/body/eval_jaxpr/psum | solution.py:57
  156.9 0.3 fusion.180
  157.2 0.3 fusion.181
  157.5 0.3 fusion.178
  157.8 0.3 fusion.179
  158.2 31.6 %all_gather.27 = f32[8,2,16,512]{3,2,1,0:T(8,128)S(1)} all-gather(f32[1,2,16,512]{3,2,1,0:T(8,128)S(1)} %maximum_select_fusion.5), channel_id=1, replica_groups=mesh['row'=8,'col'=4] {'row'}, dimensions={0}, use_global_device_ids=true | all-gather | bytes 589824 | tf_op jit(solution)/shard_map/while/body/eval_jaxpr/all_gather | solution.py:60
  190.6 0.2 fusion.70
  190.7 0.2 fusion.56
  190.9 0.2 fusion.83
  191.1 0.2 fusion.57
  191.3 38.1 %all-reduce = (f32[2,64,16]{1,2,0:T(8,128)S(1)}, f32[2,64,64]{2,1,0:T(8,128)S(1)}) all-reduce(f32[2,64,16]{1,2,0:T(8,128)S(1)} %pad_maximum_fusion.3, f32[2,64,64]{2,1,0:T(8,128)S(1)} %pad_maximum_fusion.2), channel_id=1, replica_groups=mesh['row'=8,'col'=4] {'row'}, use_global_device_ids=true, to_apply=%region_8.9 | all-reduce | flops 10240 | bytes 81920 | tf_op jit(solution)/shard_map/psum | solution.py:76
  229.9 0.2 fusion.60
  230.1 0.6 fusion.117
  231.9 0.6 fusion.112
  (61 shorter events, 3.5 us)
Async XLA Ops:
  0.6 0.7 copy-start.5
  1.4 188.5 %copy-start.4 = (f32[2,64,128]{2,1,0:T(8,128)S(1)}, f32[2,64,128]{2,1,0:T(8,128)}, u32[]{:S(2)}) copy-start(f32[2,64,128]{2,1,0:T(8,128)} %param.13) | copy-start | bytes 196612
  1.4 2.3 %copy-start = (f32[2,128,256]{2,1,0:T(8,128)S(1)}, f32[2,128,256]{2,1,0:T(8,128)}, u32[]{:S(2)}) copy-start(f32[2,128,256]{2,1,0:T(8,128)} %get-tuple-element.529) | copy-start | bytes 786436 | tf_op jit(solution)/shard_map/while
  1.4 16.7 %copy-start.2 = (f32[2,512,128]{2,1,0:T(8,128)S(1)}, f32[2,512,128]{2,1,0:T(8,128)}, u32[]{:S(2)}) copy-start(f32[2,512,128]{2,1,0:T(8,128)} %get-tuple-element.531) | copy-start | bytes 1572868 | tf_op jit(solution)/shard_map/while
  51.2 2.4 %copy-start = (f32[2,128,256]{2,1,0:T(8,128)S(1)}, f32[2,128,256]{2,1,0:T(8,128)}, u32[]{:S(2)}) copy-start(f32[2,128,256]{2,1,0:T(8,128)} %get-tuple-element.529) | copy-start | bytes 786436 | tf_op jit(solution)/shard_map/while
  51.2 14.2 %copy-start.2 = (f32[2,512,128]{2,1,0:T(8,128)S(1)}, f32[2,512,128]{2,1,0:T(8,128)}, u32[]{:S(2)}) copy-start(f32[2,512,128]{2,1,0:T(8,128)} %get-tuple-element.531) | copy-start | bytes 1572868 | tf_op jit(solution)/shard_map/while
  98.1 2.4 %copy-start.1 = (f32[2,128,256]{2,1,0:T(8,128)S(1)}, f32[2,128,256]{2,1,0:T(8,128)}, u32[]{:S(2)}) copy-start(f32[2,128,256]{2,1,0:T(8,128)} %get-tuple-element.572) | copy-start | bytes 786436 | tf_op jit(solution)/shard_map/while
  98.1 12.9 %copy-start.3 = (f32[2,512,128]{2,1,0:T(8,128)S(1)}, f32[2,512,128]{2,1,0:T(8,128)}, u32[]{:S(2)}) copy-start(f32[2,512,128]{2,1,0:T(8,128)} %get-tuple-element.573) | copy-start | bytes 1572868 | tf_op jit(solution)/shard_map/while
  143.9 2.4 %copy-start.1 = (f32[2,128,256]{2,1,0:T(8,128)S(1)}, f32[2,128,256]{2,1,0:T(8,128)}, u32[]{:S(2)}) copy-start(f32[2,128,256]{2,1,0:T(8,128)} %get-tuple-element.572) | copy-start | bytes 786436 | tf_op jit(solution)/shard_map/while
  143.9 12.9 %copy-start.3 = (f32[2,512,128]{2,1,0:T(8,128)S(1)}, f32[2,512,128]{2,1,0:T(8,128)}, u32[]{:S(2)}) copy-start(f32[2,512,128]{2,1,0:T(8,128)} %get-tuple-element.573) | copy-start | bytes 1572868 | tf_op jit(solution)/shard_map/while
